TPU v7x, 512 devices: a whole 4x4x16 slice. The times are simulated.
512 devices in a mesh: ctx: 64 (over z, y), dp: 8 (over x, core).
Axes of the slice: x: 4, y: 4, z: 16, core: 2. Of those that a mesh axis runs over, the one named last changes fastest.
Arguments:
- q_in: bfloat16 [8, 8192, 2048], P('dp', 'ctx'), may hold values from -6 to 6
- k_in: bfloat16 [8, 8192, 2048], P('dp', 'ctx'), may hold values from -6 to 6
- v_in: bfloat16 [8, 8192, 2048], P('dp', 'ctx'), may hold values from -6 to 6
- grad_out: bfloat16 [8, 8192, 2048], P('dp', 'ctx'), may hold values from -6 to 6
- short_filter: float32 [3, 3, 2048], replicated, may hold values from -3.5 to 3.5
- residue: float32 [2048, 8], replicated, may hold values from -2 to 2
- rate: float32 [8], replicated, may hold values from 0.00012207031 to 0.1
Outputs:
- mixed: bfloat16 [8, 8192, 2048], P('dp', 'ctx')
- grad_q: bfloat16 [8, 8192, 2048], P('dp', 'ctx')
- grad_k: bfloat16 [8, 8192, 2048], P('dp', 'ctx')
- grad_v: bfloat16 [8, 8192, 2048], P('dp', 'ctx')
- grad_residue: float32 [2048, 8], P('ctx')
- grad_short: float32 [3, 3, 2048], replicated
All inputs are finite; a program needn't handle non-finite values.
Results may differ from a plain program's by a relative error of at most 0.024.
Values may be sent and summed in bfloat16 or wider, within the bound.
A program may use at most 64 MiB of HBM per device.

v0:
```python
import jax
import jax.numpy as jnp
from jax import lax
from jax.sharding import PartitionSpec as P

BLOCK = 128
PRECISE = lax.Precision.HIGHEST


def passed_along(block, axis, distance):
    devices = range(lax.axis_size(axis))
    route = [(i - distance, i) for i in devices if i - distance in devices]
    return lax.ppermute(block, axis, route)


def mode_sweeps(source, cotangent, rates, columns, gains, front, behind):
    block_len = BLOCK
    block_count = source.shape[1]
    places = jnp.arange(block_len, dtype=jnp.float32)
    offset = places[:, None] - places[None, :]
    blocks = jnp.arange(block_count, dtype=jnp.float32)
    spacing = blocks[:, None] - blocks[None, :] - 1.0
    cot_f = cotangent.astype(jnp.float32)

    def one_mode(carry, item):
        conv_acc, back_acc = carry
        speed, column, start_fwd, start_back = item
        kernel = jnp.where(offset >= 0, jnp.exp(-speed * jnp.maximum(offset, 0.0)), 0.0).astype(
            jnp.bfloat16
        )
        passing = jnp.where(
            spacing >= 0, jnp.exp(-speed * block_len * jnp.maximum(spacing, 0.0)), 0.0
        )
        lead = jnp.exp(-speed * block_len * blocks)
        trail = jnp.exp(-speed * block_len * (block_count - 1.0 - blocks))
        scale_fwd = jnp.exp(-speed * (places + 1.0))
        scale_back = jnp.exp(-speed * (block_len - places))
        inside = jnp.einsum("ts,cns->cnt", kernel, source, preferred_element_type=jnp.float32)
        entering = (
            jnp.einsum("nk,ck->cn", passing, inside[..., block_len - 1], precision=PRECISE)
            + lead[None, :] * start_fwd[:, None]
        )
        forward = inside + scale_fwd[None, None, :] * entering[..., None]
        conv_acc = conv_acc + column[:, None, None] * forward
        grad_row = jnp.sum(forward * cot_f, axis=(1, 2))
        inside_back = jnp.einsum(
            "ts,cnt->cns", kernel, cotangent, preferred_element_type=jnp.float32
        )
        entering_back = (
            jnp.einsum("kn,ck->cn", passing, inside_back[..., 0], precision=PRECISE)
            + trail[None, :] * start_back[:, None]
        )
        backward = inside_back + scale_back[None, None, :] * entering_back[..., None]
        back_acc = back_acc + column[:, None, None] * backward
        return ((conv_acc, back_acc), grad_row)

    zeros_acc = jnp.zeros(source.shape, jnp.float32)
    (conv_sum, back_sum), grads = lax.scan(
        one_mode, (zeros_acc, zeros_acc), (rates, columns, front, behind)
    )
    grads = gains[:, None] * grads
    return (conv_sum, back_sum, grads.T)


def shards(q_in, k_in, v_in, grad_out, short_filter, residue, rate):
    row_count = q_in.shape[1]
    width = q_in.shape[2]
    inputs = (q_in[0], k_in[0], v_in[0])
    tails = jnp.stack([item[row_count - 2 :] for item in inputs])
    before = passed_along(tails, "ctx", 1)
    extended = [
        jnp.concatenate([before[branch], inputs[branch]], axis=0).astype(jnp.float32)
        for branch in range(3)
    ]
    shorts = []
    for branch in range(3):
        total = short_filter[branch, 0][None, :] * extended[branch][2 : 2 + row_count]
        for tap_at in range(1, 3):
            total = (
                total
                + short_filter[branch, tap_at][None, :]
                * extended[branch][2 - tap_at : 2 - tap_at + row_count]
            )
        shorts.append(total)
    query, keyed, valued = shorts
    gated = (keyed * valued).astype(jnp.bfloat16)
    cot_out = grad_out[0].astype(jnp.float32)
    d_conv = (cot_out * query).astype(jnp.bfloat16)
    gains = jnp.sqrt(1.0 - jnp.exp(-2.0 * rate))
    weights = residue * gains[None, :]
    modes = rate.shape[0]
    ctx_count = lax.axis_size("ctx")
    channel_share = width // ctx_count
    owned, incoming = (
        lax.all_to_all(gated, "ctx", split_axis=1, concat_axis=0, tiled=True),
        lax.all_to_all(d_conv, "ctx", split_axis=1, concat_axis=0, tiled=True),
    )
    total_rows = owned.shape[0]
    block_count = total_rows // BLOCK
    owned_lanes = owned.T.reshape(channel_share, block_count, BLOCK)
    incoming_lanes = incoming.T.reshape(channel_share, block_count, BLOCK)
    columns = lax.dynamic_slice_in_dim(
        weights, lax.axis_index("ctx") * channel_share, channel_share, 0
    ).T
    zero_start = jnp.zeros((modes, channel_share), jnp.float32)
    conv_sum, back_sum, partial_value = mode_sweeps(
        owned_lanes, incoming_lanes, rate, columns, gains, zero_start, zero_start
    )
    conv_rows = conv_sum.reshape(channel_share, total_rows).T.astype(jnp.bfloat16)
    back_rows = back_sum.reshape(channel_share, total_rows).T.astype(jnp.bfloat16)
    conv, d_gated = (
        lax.all_to_all(conv_rows, "ctx", split_axis=0, concat_axis=1, tiled=True),
        lax.all_to_all(back_rows, "ctx", split_axis=0, concat_axis=1, tiled=True),
    )
    grad_residue = lax.psum(partial_value, "dp")
    conv_f = conv.astype(jnp.float32)
    mixed = (query * conv_f).astype(jnp.bfloat16)
    gated_back = d_gated.astype(jnp.float32)
    d_shorts = (cot_out * conv_f, gated_back * valued, gated_back * keyed)
    heads = jnp.stack([item[:2] for item in d_shorts])
    after = passed_along(heads.astype(jnp.bfloat16), "ctx", -1).astype(heads.dtype)
    grads = []
    partial_short = []
    for branch in range(3):
        ahead_rows = jnp.concatenate([d_shorts[branch], after[branch]], axis=0)
        total = short_filter[branch, 0][None, :] * ahead_rows[0:row_count]
        for tap_at in range(1, 3):
            total = (
                total
                + short_filter[branch, tap_at][None, :] * ahead_rows[tap_at : tap_at + row_count]
            )
        grads.append(total.astype(jnp.bfloat16)[None])
        partial_short.append(
            jnp.stack(
                [
                    jnp.sum(
                        d_shorts[branch] * extended[branch][2 - tap_at : 2 - tap_at + row_count],
                        axis=0,
                    )
                    for tap_at in range(3)
                ]
            )
        )
    grad_short = lax.psum(jnp.stack(partial_short), ("ctx", "dp"))
    return (mixed[None], grads[0], grads[1], grads[2], grad_residue, grad_short)


def solution(mesh):
    placed = (
        P("dp", "ctx", None),
        P("dp", "ctx", None),
        P("dp", "ctx", None),
        P("dp", "ctx", None),
        P(),
        P(),
        P(),
    )
    return jax.shard_map(
        shards,
        mesh=mesh,
        in_specs=placed,
        out_specs=(
            P("dp", "ctx", None),
            P("dp", "ctx", None),
            P("dp", "ctx", None),
            P("dp", "ctx", None),
            P("ctx", None),
            P(),
        ),
        check_vma=False,
    )
```

profile of v0, /device:TPU:1, one launch (start us, length us, event | category | flops | bytes accessed | tf_op | source)
XLA Modules:
  0.0 703.1 jit_solution(16576350189797462453)
XLA Ops:
  9.5 4.0 collective-permute-start
  14.6 1.3 copy.33
  15.9 1.3 copy.31
  18.7 4.5 multiply_convert_fusion
  23.2 18.3 %all-to-all-start = ((bf16[128,64,32]{0,2,1:T(8,128)(2,1)}), bf16[128,64,32]{0,2,1:T(8,128)(2,1)S(1)}, u32[]{:S(2)}, u32[]{:S(2)}) async-start(bf16[128,64,32]{0,2,1:T(8,128)(2,1)} %bitcast.16), calls=%async_computation | async-start | bytes 1048576 | tf_op jit(solution)/shard_map/all_to_all | solution.py:95
  42.9 1.3 copy-done.4
  44.2 2.4 fusion.51
  46.6 24.2 %all-to-all-done = bf16[128,64,32]{0,2,1:T(8,128)(2,1)S(1)} async-done(((bf16[128,64,32]{0,2,1:T(8,128)(2,1)}), bf16[128,64,32]{0,2,1:T(8,128)(2,1)S(1)}, u32[]{:S(2)}, u32[]{:S(2)}) %all-to-all-start) | async-done | bytes 524320 | tf_op jit(solution)/shard_map/all_to_all | solution.py:95
  70.7 8.6 %all-to-all-start.1 = ((bf16[128,64,32]{0,2,1:T(8,128)(2,1)}), bf16[128,64,32]{0,2,1:T(8,128)(2,1)S(1)}, u32[]{:S(2)}, u32[]{:S(2)}) async-start(bf16[128,64,32]{0,2,1:T(8,128)(2,1)} %bitcast.20), calls=%async_computation.1 | async-start | bytes 1048576 | tf_op jit(solution)/shard_map/all_to_all | solution.py:96
  81.2 27.1 %all-to-all-done.1 = bf16[128,64,32]{0,2,1:T(8,128)(2,1)S(1)} async-done(((bf16[128,64,32]{0,2,1:T(8,128)(2,1)}), bf16[128,64,32]{0,2,1:T(8,128)(2,1)S(1)}, u32[]{:S(2)}, u32[]{:S(2)}) %all-to-all-start.1) | async-done | bytes 524320 | tf_op jit(solution)/shard_map/all_to_all | solution.py:96
  109.3 1.1 bitcast_convert_fusion
  110.5 60.8 %while.16 = (s32[]{:T(128)}, f32[32,64,128]{2,1,0:T(8,128)}, f32[32,64,128]{2,1,0:T(8,128)}, f32[8,32]{1,0:T(8,128)S(1)}, f32[8,32]{1,0:T(8,128)S(1)}, /*index=5...) while((s32[]{:T(128)}, f32[32,64,128]{2,1,0:T(8,128)}, ...), condition=%wide.region_2.3_spmd.clone.clone, body=%wide.region_0.2_spmd.clone.clone.sunk | while | flops 140759840 | bytes 12668891 | solution.py:58
  111.8 1.4 convolution_bitcast_fusion.5
  114.9 2.2 multiply_reduce_fusion.11
  118.4 1.4 convolution_bitcast_fusion.5
  121.5 3.3 multiply_reduce_fusion.11
  126.1 1.4 convolution_bitcast_fusion.5
  129.2 3.3 multiply_reduce_fusion.11
  133.8 1.4 convolution_bitcast_fusion.5
  137.0 3.3 multiply_reduce_fusion.11
  141.6 1.4 convolution_bitcast_fusion.5
  144.7 3.3 multiply_reduce_fusion.11
  149.3 1.4 convolution_bitcast_fusion.5
  152.5 3.3 multiply_reduce_fusion.11
  157.1 1.4 convolution_bitcast_fusion.5
  160.2 3.3 multiply_reduce_fusion.11
  164.8 1.4 convolution_bitcast_fusion.5
  167.9 3.3 multiply_reduce_fusion.11
  171.3 1.4 convert_element_type.94
  172.7 1.1 copy_bitcast_fusion
  173.8 9.2 %all-to-all-start.3 = ((bf16[64,128,32]{1,2,0:T(8,128)(2,1)}), bf16[64,128,32]{1,2,0:T(8,128)(2,1)}, u32[]{:S(2)}, u32[]{:S(2)}) async-start(bf16[64,128,32]{1,2,0:T(8,128)(2,1)} %copy_bitcast_fusion), calls=%async_computation.3 | async-start | bytes 1048576 | tf_op jit(solution)/shard_map/all_to_all | solution.py:113
  183.1 1.1 copy_bitcast_fusion.1
  184.3 27.9 %all-to-all-done.3 = bf16[64,128,32]{1,2,0:T(8,128)(2,1)} async-done(((bf16[64,128,32]{1,2,0:T(8,128)(2,1)}), bf16[64,128,32]{1,2,0:T(8,128)(2,1)}, u32[]{:S(2)}, u32[]{:S(2)}) %all-to-all-start.3) | async-done | bytes 524320 | tf_op jit(solution)/shard_map/all_to_all | solution.py:113
  212.1 8.9 %all-to-all-start.2 = ((bf16[64,128,32]{1,2,0:T(8,128)(2,1)}), bf16[64,128,32]{1,2,0:T(8,128)(2,1)}, u32[]{:S(2)}, u32[]{:S(2)}) async-start(bf16[64,128,32]{1,2,0:T(8,128)(2,1)} %copy_bitcast_fusion.1), calls=%async_computation.2 | async-start | bytes 1048576 | tf_op jit(solution)/shard_map/all_to_all | solution.py:112
  221.2 14.6 %psum.14 = f32[32,8]{0,1:T(8,128)} all-reduce(f32[32,8]{0,1:T(8,128)S(1)} %multiply_bitcast_fusion), channel_id=1, replica_groups=mesh['ctx'=64,'dp'=8] {'dp'}, use_global_device_ids=true, to_apply=%region_3.4 | all-reduce | flops 256 | bytes 2048 | tf_op jit(solution)/shard_map/psum | solution.py:115
  235.8 6.3 multiply_reduce_fusion.6
  243.9 1.2 copy.40
  246.0 1.2 copy.41
  247.3 2.9 all-to-all-done.2
  250.2 3.0 multiply_reduce_fusion.9
  253.5 1.3 collective-permute-start.1
  256.6 1.5 collective-permute-done.1
  260.4 2.2 fusion.76
  262.6 2.2 fusion.75
  264.8 2.2 fusion.74
  266.9 1.0 copy.46
  270.0 424.7 %all-reduce.2.cloned.1.call-done = f32[3,3,2048]{2,1,0:T(4,128)} async-done(((f32[3,3,2048]{2,1,0:T(4,128)}), f32[3,3,2048]{2,1,0:T(4,128)}) %all-reduce.2.cloned.1.call-update) | async-done | bytes 73744 | tf_op jit(solution)/shard_map/psum | solution.py:144
  694.7 1.5 copy.80
  (167 shorter events, 36.5 us)
Async XLA Ops:
  9.5 7.7 %collective-permute-start = (bf16[3,2,2048]{2,1,0:T(2,128)(2,1)S(1)}, bf16[3,2,2048]{2,1,0:T(2,128)(2,1)S(1)}, u32[]{:S(2)}, u32[]{:S(2)}) collective-permute-start(bf16[3,2,2048]{2,1,0:T(2,128)(2,1)S(1)} %pad_maximum_fusion.4), channel_id=1, source_target_pairs={{0,8},{8,16},{16,24},{24,32},{32,40},{40,48},{48,56},{56,64},{64,7... | collective-permute-start | bytes 73736 | tf_op jit(solution)/shard_map/ppermute | solution.py:13
  18.7 4.5 copy-start.1
  18.7 4.5 copy-start.3
  18.7 22.8 %copy-start.13 = (bf16[1,128,2048]{2,1,0:T(8,128)(2,1)S(1)}, bf16[1,128,2048]{2,1,0:T(8,128)(2,1)}, u32[]{:S(2)}) copy-start(bf16[1,128,2048]{2,1,0:T(8,128)(2,1)} %param.9) | copy-start | bytes 1572868
  23.2 18.6 %copy-start.14 = (bf16[1,128,2048]{2,1,0:T(8,128)(2,1)S(1)}, bf16[1,128,2048]{2,1,0:T(8,128)(2,1)}, u32[]{:S(2)}) copy-start(bf16[1,128,2048]{2,1,0:T(8,128)(2,1)} %param.12) | copy-start | bytes 1572868
  23.2 47.5 %all-to-all-start = ((bf16[128,64,32]{0,2,1:T(8,128)(2,1)}), bf16[128,64,32]{0,2,1:T(8,128)(2,1)S(1)}, u32[]{:S(2)}, u32[]{:S(2)}) async-start(bf16[128,64,32]{0,2,1:T(8,128)(2,1)} %bitcast.16), calls=%async_computation | async-start | bytes 1048576 | tf_op jit(solution)/shard_map/all_to_all | solution.py:95
  42.1 4.5 copy-start.11
  42.8 1.4 copy-start.4
  44.2 35.2 %copy-start.15 = (f32[8]{0:T(128)S(1)}, f32[8]{0:T(128)}, u32[]{:S(2)}) copy-start(f32[8]{0:T(128)} %param.15) | copy-start | bytes 100
  70.7 37.6 %all-to-all-start.1 = ((bf16[128,64,32]{0,2,1:T(8,128)(2,1)}), bf16[128,64,32]{0,2,1:T(8,128)(2,1)S(1)}, u32[]{:S(2)}, u32[]{:S(2)}) async-start(bf16[128,64,32]{0,2,1:T(8,128)(2,1)} %bitcast.20), calls=%async_computation.1 | async-start | bytes 1048576 | tf_op jit(solution)/shard_map/all_to_all | solution.py:96
  111.7 2.0 copy-start.6
  118.3 2.0 copy-start.6
  126.1 2.0 copy-start.6
  133.8 2.0 copy-start.6
  141.6 2.0 copy-start.6
  149.3 2.0 copy-start.6
  157.0 2.0 copy-start.6
  164.8 2.0 copy-start.6
  171.3 11.8 %copy-start = (f32[32,64,128]{2,1,0:T(8,128)S(1)}, f32[32,64,128]{2,1,0:T(8,128)}, u32[]{:S(2)}) copy-start(f32[32,64,128]{2,1,0:T(8,128)} %get-tuple-element.87) | copy-start | bytes 3145732
  173.8 38.3 %all-to-all-start.3 = ((bf16[64,128,32]{1,2,0:T(8,128)(2,1)}), bf16[64,128,32]{1,2,0:T(8,128)(2,1)}, u32[]{:S(2)}, u32[]{:S(2)}) async-start(bf16[64,128,32]{1,2,0:T(8,128)(2,1)} %copy_bitcast_fusion), calls=%async_computation.3 | async-start | bytes 1048576 | tf_op jit(solution)/shard_map/all_to_all | solution.py:113
  183.0 52.7 %copy-start.2 = (f32[130,2048]{0,1:T(8,128)S(1)}, f32[130,2048]{0,1:T(8,128)}, u32[]{:S(2)}) copy-start(f32[130,2048]{0,1:T(8,128)} %copy-done.1) | copy-start | bytes 3194884
  212.1 38.0 %all-to-all-start.2 = ((bf16[64,128,32]{1,2,0:T(8,128)(2,1)}), bf16[64,128,32]{1,2,0:T(8,128)(2,1)}, u32[]{:S(2)}, u32[]{:S(2)}) async-start(bf16[64,128,32]{1,2,0:T(8,128)(2,1)} %copy_bitcast_fusion.1), calls=%async_computation.2 | async-start | bytes 1048576 | tf_op jit(solution)/shard_map/all_to_all | solution.py:112
  221.0 473.7 %all-reduce.2.cloned.1.call-start = ((), (), s32[]{:S(2)}) async-start(), calls=%async_computation.4 | async-start | bytes 196608 | tf_op jit(solution)/shard_map/psum | solution.py:144
  242.1 1.0 copy-start.7
  242.1 8.1 %copy-start.9 = (f32[128,2048]{0,1:T(8,128)}, f32[128,2048]{0,1:T(8,128)S(1)}, u32[]{:S(2)}) copy-start(f32[128,2048]{0,1:T(8,128)S(1)} %get-tuple-element.228) | copy-start | bytes 3145732
  242.1 8.0 %copy-start.5 = (f32[130,2048]{0,1:T(8,128)S(1)}, f32[130,2048]{0,1:T(8,128)}, u32[]{:S(2)}) copy-start(f32[130,2048]{0,1:T(8,128)} %copy-done.4) | copy-start | bytes 3194884
  253.2 2.4 copy-start.12
  253.5 4.6 collective-permute-start.1
  259.1 1.2 copy-start.10
  259.4 3.2 copy-start.8
Sparse Core Ops, SparseCore 0:
  255.7 438.9 all-reduce.1
where the time goes:
time: 705 us; the launch traced here: 703 us
  waiting for transfers between devices  508 us (72%)
  other arithmetic  54 us (8%)
  starting transfers between devices  50.4 us (7%)
  local copies, waits for them, and re-layouts  39.1 us (6%)
  matrix products  16.5 us (2%)
  blocking collectives  14.6 us (2%)
  between operations  14.5 us (2%)
    psum x1, waiting for transfers between devices, shards(): grad_short = lax.psum(jnp.stack(partial_short), ('ctx', 'dp'))  425 us
    all_to_all x1, waiting for transfers between devices, shards(): lax.all_to_all(back_rows, 'ctx', split_axis=0, concat_axis=1, tiled=True)  27.9 us
    all_to_all x1, waiting for transfers between devices, shards(): lax.all_to_all(d_conv, 'ctx', split_axis=1, concat_axis=0, tiled=True)  27.1 us
    reduce_sum x8, other arithmetic, one_mode(): grad_row = jnp.sum(forward * cot_f, axis=(1, 2))  25.3 us
    all_to_all x1, waiting for transfers between devices, shards(): lax.all_to_all(gated, 'ctx', split_axis=1, concat_axis=0, tiled=True)  24.2 us
    all_to_all x1, starting transfers between devices, shards(): lax.all_to_all(gated, 'ctx', split_axis=1, concat_axis=0, tiled=True)  18.3 us
    unnamed x46, local copies, waits for them, and re-layouts  15 us
    psum x1, blocking collectives, shards(): grad_residue = lax.psum(partial_value, 'dp')  14.6 us
  transfers between devices with their start and end apart: 7, of which 6 were waited for; matrix products, arithmetic and copies ran while one was open for 5% of the time, Pallas kernels for 0%

commit v1 on v0

--- a/solution.py
+++ b/solution.py
@@ -2,6 +2,7 @@
 import jax.numpy as jnp
 from jax import lax
 from jax.sharding import PartitionSpec as P
+from jax.lax import psum
 
 BLOCK = 128
 PRECISE = lax.Precision.HIGHEST
@@ -141,7 +142,9 @@
                 ]
             )
         )
-    grad_short = lax.psum(jnp.stack(partial_short), ("ctx", "dp"))
+    vec = jnp.stack(partial_short)
+    response = psum(vec, axis_name="dp")
+    grad_short = psum(response, axis_name="ctx")
     return (mixed[None], grads[0], grads[1], grads[2], grad_residue, grad_short)
 
 

time: 705 us -> 598 us (0.85); the launches traced: 703 us -> 587 us
  waiting for transfers between devices: 508 us -> 390 us
    psum x1 -> x2, waiting for transfers between devices: 425 us -> 307 us  [the longest x1 247 us: shards(): grad_short = psum(response, axis_name='ctx')]
    unnamed x46 -> x52, local copies, waits for them, and re-layouts: 15 us -> 15.1 us
  transfers between devices with their start and end apart: 7 -> 8, of which waited for: 6 -> 7; matrix products, arithmetic and copies ran while one was open for 5% -> 6% of each run, Pallas kernels for 0% -> 0%
where the time goes in v1:
time: 598 us; the launch traced here: 587 us
  waiting for transfers between devices  390 us (65%)
  other arithmetic  55.6 us (9%)
  starting transfers between devices  50.5 us (8%)
  local copies, waits for them, and re-layouts  39.1 us (7%)
  matrix products  16.5 us (3%)
  blocking collectives  14.6 us (2%)
  between operations  14.5 us (2%)
    psum x1, waiting for transfers between devices, shards(): grad_short = psum(response, axis_name='ctx')  247 us
    psum x1, waiting for transfers between devices, shards(): response = psum(vec, axis_name='dp')  59.5 us
    all_to_all x1, waiting for transfers between devices, shards(): lax.all_to_all(back_rows, 'ctx', split_axis=0, concat_axis=1, tiled=True)  27.9 us
    all_to_all x1, waiting for transfers between devices, shards(): lax.all_to_all(d_conv, 'ctx', split_axis=1, concat_axis=0, tiled=True)  27.1 us
    reduce_sum x8, other arithmetic, one_mode(): grad_row = jnp.sum(forward * cot_f, axis=(1, 2))  25.3 us
    all_to_all x1, waiting for transfers between devices, shards(): lax.all_to_all(gated, 'ctx', split_axis=1, concat_axis=0, tiled=True)  24.2 us
    all_to_all x1, starting transfers between devices, shards(): lax.all_to_all(gated, 'ctx', split_axis=1, concat_axis=0, tiled=True)  18.3 us
    unnamed x52, local copies, waits for them, and re-layouts  15.1 us
  transfers between devices with their start and end apart: 8, of which 7 were waited for; matrix products, arithmetic and copies ran while one was open for 6% of the time, Pallas kernels for 0%

profile of v1, /device:TPU:1, one launch (start us, length us, event | category | flops | bytes accessed | tf_op | source)
XLA Modules:
  0.0 586.9 jit_solution(16462427615787028086)
XLA Ops:
  9.5 4.0 collective-permute-start
  14.6 1.3 copy.33
  15.9 1.3 copy.31
  18.7 4.5 multiply_convert_fusion
  23.2 18.3 %all-to-all-start = ((bf16[128,64,32]{0,2,1:T(8,128)(2,1)}), bf16[128,64,32]{0,2,1:T(8,128)(2,1)S(1)}, u32[]{:S(2)}, u32[]{:S(2)}) async-start(bf16[128,64,32]{0,2,1:T(8,128)(2,1)} %bitcast.16), calls=%async_computation | async-start | bytes 1048576 | tf_op jit(solution)/shard_map/all_to_all | solution.py:96
  42.9 1.3 copy-done.4
  44.2 2.4 fusion.51
  46.6 24.2 %all-to-all-done = bf16[128,64,32]{0,2,1:T(8,128)(2,1)S(1)} async-done(((bf16[128,64,32]{0,2,1:T(8,128)(2,1)}), bf16[128,64,32]{0,2,1:T(8,128)(2,1)S(1)}, u32[]{:S(2)}, u32[]{:S(2)}) %all-to-all-start) | async-done | bytes 524320 | tf_op jit(solution)/shard_map/all_to_all | solution.py:96
  70.7 8.6 %all-to-all-start.1 = ((bf16[128,64,32]{0,2,1:T(8,128)(2,1)}), bf16[128,64,32]{0,2,1:T(8,128)(2,1)S(1)}, u32[]{:S(2)}, u32[]{:S(2)}) async-start(bf16[128,64,32]{0,2,1:T(8,128)(2,1)} %bitcast.20), calls=%async_computation.1 | async-start | bytes 1048576 | tf_op jit(solution)/shard_map/all_to_all | solution.py:97
  81.2 27.1 %all-to-all-done.1 = bf16[128,64,32]{0,2,1:T(8,128)(2,1)S(1)} async-done(((bf16[128,64,32]{0,2,1:T(8,128)(2,1)}), bf16[128,64,32]{0,2,1:T(8,128)(2,1)S(1)}, u32[]{:S(2)}, u32[]{:S(2)}) %all-to-all-start.1) | async-done | bytes 524320 | tf_op jit(solution)/shard_map/all_to_all | solution.py:97
  109.3 1.1 bitcast_convert_fusion
  110.5 60.8 %while.16 = (s32[]{:T(128)}, f32[32,64,128]{2,1,0:T(8,128)}, f32[32,64,128]{2,1,0:T(8,128)}, f32[8,32]{1,0:T(8,128)S(1)}, f32[8,32]{1,0:T(8,128)S(1)}, /*index=5...) while((s32[]{:T(128)}, f32[32,64,128]{2,1,0:T(8,128)}, ...), condition=%wide.region_2.3_spmd.clone.clone, body=%wide.region_0.2_spmd.clone.clone.sunk | while | flops 140759840 | bytes 12668891 | solution.py:59
  111.8 1.4 convolution_bitcast_fusion.5
  114.9 2.2 multiply_reduce_fusion.11
  118.4 1.4 convolution_bitcast_fusion.5
  121.5 3.3 multiply_reduce_fusion.11
  126.1 1.4 convolution_bitcast_fusion.5
  129.2 3.3 multiply_reduce_fusion.11
  133.8 1.4 convolution_bitcast_fusion.5
  137.0 3.3 multiply_reduce_fusion.11
  141.6 1.4 convolution_bitcast_fusion.5
  144.7 3.3 multiply_reduce_fusion.11
  149.3 1.4 convolution_bitcast_fusion.5
  152.4 3.3 multiply_reduce_fusion.11
  157.1 1.4 convolution_bitcast_fusion.5
  160.2 3.3 multiply_reduce_fusion.11
  164.8 1.4 convolution_bitcast_fusion.5
  167.9 3.3 multiply_reduce_fusion.11
  171.3 1.4 convert_element_type.94
  172.7 1.1 copy_bitcast_fusion
  173.8 9.2 %all-to-all-start.3 = ((bf16[64,128,32]{1,2,0:T(8,128)(2,1)}), bf16[64,128,32]{1,2,0:T(8,128)(2,1)}, u32[]{:S(2)}, u32[]{:S(2)}) async-start(bf16[64,128,32]{1,2,0:T(8,128)(2,1)} %copy_bitcast_fusion), calls=%async_computation.3 | async-start | bytes 1048576 | tf_op jit(solution)/shard_map/all_to_all | solution.py:114
  183.1 1.1 copy_bitcast_fusion.1
  184.3 27.9 %all-to-all-done.3 = bf16[64,128,32]{1,2,0:T(8,128)(2,1)} async-done(((bf16[64,128,32]{1,2,0:T(8,128)(2,1)}), bf16[64,128,32]{1,2,0:T(8,128)(2,1)}, u32[]{:S(2)}, u32[]{:S(2)}) %all-to-all-start.3) | async-done | bytes 524320 | tf_op jit(solution)/shard_map/all_to_all | solution.py:114
  212.1 8.9 %all-to-all-start.2 = ((bf16[64,128,32]{1,2,0:T(8,128)(2,1)}), bf16[64,128,32]{1,2,0:T(8,128)(2,1)}, u32[]{:S(2)}, u32[]{:S(2)}) async-start(bf16[64,128,32]{1,2,0:T(8,128)(2,1)} %copy_bitcast_fusion.1), calls=%async_computation.2 | async-start | bytes 1048576 | tf_op jit(solution)/shard_map/all_to_all | solution.py:113
  221.2 14.6 %psum.21 = f32[32,8]{0,1:T(8,128)} all-reduce(f32[32,8]{0,1:T(8,128)S(1)} %multiply_bitcast_fusion), channel_id=1, replica_groups=mesh['ctx'=64,'dp'=8] {'dp'}, use_global_device_ids=true, to_apply=%region_3.4 | all-reduce | flops 256 | bytes 2048 | tf_op jit(solution)/shard_map/psum | solution.py:116
  235.8 6.2 %multiply_reduce_fusion.6 = (f32[2048]{0:T(1024)S(1)}, f32[2048]{0:T(1024)S(1)}, f32[2048]{0:T(1024)S(1)}, f32[128,2048]{0,1:T(8,128)S(1)}, f32[2048]{0:T(1024)S...) fusion(f32[130,2048]{0,1:T(8,128)S(1)} %copy-done.2, f32[128,2048]{0,1:T(8,128)} %get-tuple-element.211, ...), kind=kLoop, calls=%fused_computation.106 | loop fusion | flops 3919872 | bytes 11059200 | tf_op jit(solution)/shard_map/reduce_sum | solution.py:137
  243.9 1.2 copy.40
  246.0 1.2 copy.41
  247.2 2.9 all-to-all-done.2
  250.1 3.0 multiply_reduce_fusion.9
  253.5 1.3 collective-permute-start.1
  256.6 1.4 collective-permute-done.1
  260.4 2.7 fusion.76
  263.1 2.8 fusion.75
  265.9 59.5 %all-reduce.3.cloned.1.call-done = f32[3,3,2048]{2,1,0:T(4,128)} async-done(((f32[3,3,2048]{2,1,0:T(4,128)}), f32[3,3,2048]{2,1,0:T(4,128)}) %all-reduce.3.cloned.1.call-update) | async-done | bytes 73744 | tf_op jit(solution)/shard_map/psum | solution.py:146
  325.4 2.8 fusion.74
  331.2 247.4 %all-reduce.5.cloned.1.call-done = f32[3,3,2048]{2,1,0:T(4,128)} async-done(((f32[3,3,2048]{2,1,0:T(4,128)}), f32[3,3,2048]{2,1,0:T(4,128)}) %all-reduce.5.cloned.1.call-update) | async-done | bytes 73744 | tf_op jit(solution)/shard_map/psum | solution.py:147
  578.6 1.5 copy.81
  (176 shorter events, 37.6 us)
Async XLA Ops:
  9.5 7.7 %collective-permute-start = (bf16[3,2,2048]{2,1,0:T(2,128)(2,1)S(1)}, bf16[3,2,2048]{2,1,0:T(2,128)(2,1)S(1)}, u32[]{:S(2)}, u32[]{:S(2)}) collective-permute-start(bf16[3,2,2048]{2,1,0:T(2,128)(2,1)S(1)} %pad_maximum_fusion.4), channel_id=1, source_target_pairs={{0,8},{8,16},{16,24},{24,32},{32,40},{40,48},{48,56},{56,64},{64,7... | collective-permute-start | bytes 73736 | tf_op jit(solution)/shard_map/ppermute | solution.py:14
  18.7 4.5 copy-start.1
  18.7 4.5 copy-start.3
  18.7 22.8 %copy-start.16 = (bf16[1,128,2048]{2,1,0:T(8,128)(2,1)S(1)}, bf16[1,128,2048]{2,1,0:T(8,128)(2,1)}, u32[]{:S(2)}) copy-start(bf16[1,128,2048]{2,1,0:T(8,128)(2,1)} %param.9) | copy-start | bytes 1572868
  23.2 18.6 %copy-start.17 = (bf16[1,128,2048]{2,1,0:T(8,128)(2,1)S(1)}, bf16[1,128,2048]{2,1,0:T(8,128)(2,1)}, u32[]{:S(2)}) copy-start(bf16[1,128,2048]{2,1,0:T(8,128)(2,1)} %param.12) | copy-start | bytes 1572868
  23.2 47.5 %all-to-all-start = ((bf16[128,64,32]{0,2,1:T(8,128)(2,1)}), bf16[128,64,32]{0,2,1:T(8,128)(2,1)S(1)}, u32[]{:S(2)}, u32[]{:S(2)}) async-start(bf16[128,64,32]{0,2,1:T(8,128)(2,1)} %bitcast.16), calls=%async_computation | async-start | bytes 1048576 | tf_op jit(solution)/shard_map/all_to_all | solution.py:96
  42.1 4.5 copy-start.11
  42.9 1.3 copy-start.4
  44.2 35.2 %copy-start.18 = (f32[8]{0:T(128)S(1)}, f32[8]{0:T(128)}, u32[]{:S(2)}) copy-start(f32[8]{0:T(128)} %param.15) | copy-start | bytes 100
  70.7 37.6 %all-to-all-start.1 = ((bf16[128,64,32]{0,2,1:T(8,128)(2,1)}), bf16[128,64,32]{0,2,1:T(8,128)(2,1)S(1)}, u32[]{:S(2)}, u32[]{:S(2)}) async-start(bf16[128,64,32]{0,2,1:T(8,128)(2,1)} %bitcast.20), calls=%async_computation.1 | async-start | bytes 1048576 | tf_op jit(solution)/shard_map/all_to_all | solution.py:97
  111.7 2.0 copy-start.6
  118.3 2.0 copy-start.6
  126.1 2.0 copy-start.6
  133.8 2.0 copy-start.6
  141.5 2.0 copy-start.6
  149.3 2.0 copy-start.6
  157.0 2.0 copy-start.6
  164.8 2.0 copy-start.6
  171.3 11.8 %copy-start = (f32[32,64,128]{2,1,0:T(8,128)S(1)}, f32[32,64,128]{2,1,0:T(8,128)}, u32[]{:S(2)}) copy-start(f32[32,64,128]{2,1,0:T(8,128)} %get-tuple-element.87) | copy-start | bytes 3145732
  173.8 38.3 %all-to-all-start.3 = ((bf16[64,128,32]{1,2,0:T(8,128)(2,1)}), bf16[64,128,32]{1,2,0:T(8,128)(2,1)}, u32[]{:S(2)}, u32[]{:S(2)}) async-start(bf16[64,128,32]{1,2,0:T(8,128)(2,1)} %copy_bitcast_fusion), calls=%async_computation.3 | async-start | bytes 1048576 | tf_op jit(solution)/shard_map/all_to_all | solution.py:114
  183.0 52.7 %copy-start.2 = (f32[130,2048]{0,1:T(8,128)S(1)}, f32[130,2048]{0,1:T(8,128)}, u32[]{:S(2)}) copy-start(f32[130,2048]{0,1:T(8,128)} %copy-done.1) | copy-start | bytes 3194884
  212.1 38.0 %all-to-all-start.2 = ((bf16[64,128,32]{1,2,0:T(8,128)(2,1)}), bf16[64,128,32]{1,2,0:T(8,128)(2,1)}, u32[]{:S(2)}, u32[]{:S(2)}) async-start(bf16[64,128,32]{1,2,0:T(8,128)(2,1)} %copy_bitcast_fusion.1), calls=%async_computation.2 | async-start | bytes 1048576 | tf_op jit(solution)/shard_map/all_to_all | solution.py:113
  221.0 104.3 %all-reduce.3.cloned.1.call-start = ((), (), s32[]{:S(2)}) async-start(), calls=%async_computation.4 | async-start | bytes 196608 | tf_op jit(solution)/shard_map/psum | solution.py:146
  242.0 1.0 copy-start.7
  242.0 8.1 %copy-start.9 = (f32[128,2048]{0,1:T(8,128)}, f32[128,2048]{0,1:T(8,128)S(1)}, u32[]{:S(2)}) copy-start(f32[128,2048]{0,1:T(8,128)S(1)} %get-tuple-element.228) | copy-start | bytes 3145732
  242.0 8.1 %copy-start.5 = (f32[130,2048]{0,1:T(8,128)S(1)}, f32[130,2048]{0,1:T(8,128)}, u32[]{:S(2)}) copy-start(f32[130,2048]{0,1:T(8,128)} %copy-done.4) | copy-start | bytes 3194884
  253.1 2.5 copy-start.15
  253.5 4.6 collective-permute-start.1
  255.6 323.0 %all-reduce.5.cloned.1.call-start = ((), (), s32[]{:S(2)}) async-start(), calls=%async_computation.5 | async-start | bytes 196608 | tf_op jit(solution)/shard_map/psum | solution.py:147
  259.1 1.2 copy-start.10
  259.4 3.8 copy-start.8
  265.9 62.3 %copy-start.12 = (bf16[1,128,2048]{1,2,0:T(8,128)(2,1)S(1)}, bf16[1,128,2048]{1,2,0:T(8,128)(2,1)}, u32[]{:S(2)}) copy-start(bf16[1,128,2048]{1,2,0:T(8,128)(2,1)} %fusion.76) | copy-start | bytes 1572868
  265.9 63.3 %copy-start.13 = (bf16[1,128,2048]{1,2,0:T(8,128)(2,1)S(1)}, bf16[1,128,2048]{1,2,0:T(8,128)(2,1)}, u32[]{:S(2)}) copy-start(bf16[1,128,2048]{1,2,0:T(8,128)(2,1)} %fusion.75) | copy-start | bytes 1572868
  328.1 2.0 copy-start.14
Sparse Core Ops, SparseCore 0:
  255.7 69.5 all-reduce.2
  329.1 249.3 all-reduce.4
